TPU v7x, 32 devices: a whole 2x2x4 slice. The times are simulated.
32 devices in a mesh: replica: 8 (over z, y), shard: 4 (over x, core).
Axes of the slice: x: 2, y: 2, z: 4, core: 2. Of those that a mesh axis runs over, the one named last changes fastest.
Arguments:
- block_input: bfloat16 [16, 256, 2048], P('replica', 'shard'), may hold values from -6 to 6
- segment_ids: int32 [16, 256], P('replica'), may hold values from 0 to 3, never falling along the last dimension, each value on 1 to 192 neighbouring positions
- norm_gain: bfloat16 [2048], P('shard'), may hold values from 0.5 to 1.5
- w_in: bfloat16 [2048, 8192], P(None, 'shard'), may hold values from -0.125 to 0.125
- conv_weight: bfloat16 [4, 4096], P(None, 'shard'), may hold values from -3 to 3
- conv_bias: bfloat16 [4096], P('shard'), may hold values from -1.5 to 1.5
- x_proj: bfloat16 [160, 4096], P(None, 'shard'), may hold values from -1 to 1
- dt_proj: bfloat16 [128, 4096], P(None, 'shard'), may hold values from -0.5 to 0.5
- dt_bias: bfloat16 [4096], P('shard'), may hold values from -4 to 1
- d_skip: bfloat16 [4096], P('shard'), may hold values from 0.5 to 1.5
- out_proj: bfloat16 [4096, 2048], P(None, 'shard'), may hold values from -0.1875 to 0.1875
- out_grad: bfloat16 [16, 256, 2048], P('replica', 'shard'), may hold values from -6 to 6
Outputs:
- block_output: bfloat16 [16, 256, 2048], P('replica', 'shard')
- input_grad: bfloat16 [16, 256, 2048], P('replica', 'shard')
- grad_norm_gain: float32 [2048], P('shard')
- grad_w_in: float32 [2048, 8192], P('replica', 'shard')
- grad_conv_weight: float32 [4, 4096], P(None, 'shard')
- grad_conv_bias: float32 [4096], P('shard')
- grad_x_proj: float32 [160, 4096], P(None, 'shard')
- grad_dt_proj: float32 [128, 4096], P(None, 'shard')
- grad_dt_bias: float32 [4096], P('shard')
- grad_d_skip: float32 [4096], P('shard')
- grad_out_proj: float32 [4096, 2048], P('replica', 'shard')
Inputs may be any that keep to these rules, and one draw needn't show every extreme that they name: `segment_ids`: within each sequence the ids never fall; each of the 4 documents holds 1 to 192 tokens and one holds exactly 192.
All inputs are finite; a program needn't handle non-finite values.
Results may differ from a plain program's by a relative error of at most 0.012.
The roundings to bfloat16 on the way count: a program that leaves them out, or rounds other values in their place, can miss the bound.
Values may be sent and summed in bfloat16 or wider, within the bound.
A program may use at most 240 MiB of HBM per device.

v0:
```python
import jax
import jax.numpy as jnp
from jax import lax
from jax.sharding import PartitionSpec as P

KW = 4
EPS = 1e-05
block_len = 16


def passed_along(block, axis, distance):
    devices = range(lax.axis_size(axis))
    route = [(i - distance, i) for i in devices if i - distance in devices]
    return lax.ppermute(block, axis, route)


def carried_in(value, axis, join, neutral):
    count, mine = (lax.axis_size(axis), lax.axis_index(axis))
    pieces = jax.tree.map(lambda part: lax.all_gather(part, axis), value)
    total = jax.tree.map(
        lambda part, zero: jnp.full_like(part, 0) + jnp.asarray(zero, part.dtype), value, neutral
    )

    def hop(position, total):
        longer = join(total, jax.tree.map(lambda part: part[position], pieces))
        return jax.tree.map(lambda new, old: jnp.where(position < mine, new, old), longer, total)

    return lax.fori_loop(0, count - 1, hop, total)


def entering(shard, axis, join, neutral):
    count = lax.axis_size(axis)
    place = lax.axis_index(axis)
    ahead = count - 1 - place
    gathered = jax.tree.map(
        lambda a, kind: lax.all_gather(a.astype(kind), axis), shard, (jnp.bfloat16, jnp.bfloat16)
    )
    state = jax.tree.map(lambda a, e: jnp.zeros_like(a) + jnp.asarray(e, a.dtype), shard, neutral)

    def one(hop, state):
        source = count - 1 - hop
        return join(
            state,
            jax.tree.map(
                lambda a, own: lax.dynamic_index_in_dim(a, source, 0, False).astype(own.dtype),
                gathered,
                shard,
            ),
        )

    return lax.fori_loop(0, ahead, one, state)


def rows_dot(first_op, second_op):
    return jnp.dot(first_op, second_op, preferred_element_type=jnp.float32)


def inner_dot(first_op, second_op):
    return lax.dot_general(
        first_op, second_op, (((0,), (0,)), ((), ())), preferred_element_type=jnp.float32
    )


def outer_dot(first_op, second_op):
    return lax.dot_general(
        first_op, second_op, (((1,), (1,)), ((), ())), preferred_element_type=jnp.float32
    )


def silu_slope(values):
    sig_val = jax.nn.sigmoid(values)
    return sig_val + values * sig_val * (1.0 - sig_val)


def decay_of(rate_row, key_row, keep_val):
    return (1.0 - rate_row[:, None] * (key_row * key_row)[None, :]) * keep_val


def block_forward(carried, pieces):
    rate_blk, conv_blk, key_blk, query_blk, keep_blk = pieces
    outputs = []
    for t in range(rate_blk.shape[0]):
        decay_now = decay_of(rate_blk[t], key_blk[t], keep_blk[t])
        carried = decay_now * carried + (rate_blk[t] * conv_blk[t])[:, None] * key_blk[t][None, :]
        outputs.append(jnp.sum(carried * query_blk[t][None, :], axis=1))
    return (carried, jnp.stack(outputs))


def block_product(carried, pieces):
    total_decay, local_state = carried
    rate_blk, conv_blk, key_blk, query_blk, keep_blk = pieces
    for t in range(rate_blk.shape[0]):
        decay_now = decay_of(rate_blk[t], key_blk[t], keep_blk[t])
        total_decay = decay_now * total_decay
        local_state = (
            decay_now * local_state + (rate_blk[t] * conv_blk[t])[:, None] * key_blk[t][None, :]
        )
    return ((total_decay, local_state), None)


def block_record(carried, pieces):
    end_state, outputs = block_forward(carried, pieces)
    return (end_state, (carried, outputs))


def block_adjoint(adjoint, pieces):
    rate_blk, key_blk, query_blk, keep_blk, dout_blk = pieces
    for t in reversed(range(rate_blk.shape[0])):
        adjoint = adjoint + dout_blk[t][:, None] * query_blk[t][None, :]
        adjoint = decay_of(rate_blk[t], key_blk[t], keep_blk[t]) * adjoint
    return (adjoint, None)


def block_backward(grad_state, inputs):
    start_state = inputs[0]
    pieces = inputs[1:6]
    dout_blk = inputs[6]
    pullback = jax.vjp(block_forward, start_state, pieces)[1]
    grad_start, grad_pieces = pullback((grad_state, dout_blk))
    return (grad_start, grad_pieces[:4])


def chain_combine(earlier, later):
    return (earlier[0] * later[0], later[0] * earlier[1] + later[1])


def conv_apply(extended, conv_w, conv_b, tap_masks):
    tok_local = extended.shape[0] - (KW - 1)
    conv_sum = conv_b + conv_w[KW - 1] * extended[KW - 1 :]
    for j in range(KW - 1):
        conv_sum = (
            conv_sum + conv_w[j] * extended[j : j + tok_local] * tap_masks[KW - 2 - j][:, None]
        )
    return conv_sum


def one_batch(weights, x_rows, cot_rows, seg_window):
    norm_gain, w_in, conv_weight, conv_bias, x_proj, dt_proj, dt_bias, d_skip, out_proj = weights
    tok_local = x_rows.shape[0]
    width = d_skip.shape[0]
    rank = dt_proj.shape[0]
    state_dim = (x_proj.shape[0] - rank) // 2
    count_blocks = tok_local // block_len
    x_vals = x_rows.astype(jnp.float32)
    inv_rms = lax.rsqrt(jnp.mean(x_vals * x_vals, axis=1, keepdims=True) + EPS)
    gain_vals = norm_gain.astype(jnp.float32)
    normed = (x_vals * inv_rms * gain_vals).astype(jnp.bfloat16)
    mixed = rows_dot(normed, w_in).astype(jnp.bfloat16)
    x_part = mixed[:, :width]
    z_vals = mixed[:, width:].astype(jnp.float32)
    edge_rows = passed_along(x_part[tok_local - (KW - 1) :], "shard", 1)
    extended = jnp.concatenate([edge_rows, x_part], axis=0).astype(jnp.float32)
    tap_masks = [
        (seg_window[KW - 1 - d : KW - 1 - d + tok_local] == seg_window[KW - 1 :]).astype(
            jnp.float32
        )
        for d in range(1, KW)
    ]
    keep_rows = tap_masks[0]
    conv_w = conv_weight.astype(jnp.float32)
    conv_b = conv_bias.astype(jnp.float32)
    conv_pre = conv_apply(extended, conv_w, conv_b, tap_masks)
    conv_out = jax.nn.silu(conv_pre).astype(jnp.bfloat16)
    conv_vals = conv_out.astype(jnp.float32)
    proj_vals = outer_dot(conv_out, x_proj)
    dt_low = proj_vals[:, :rank].astype(jnp.bfloat16)
    key_rows = proj_vals[:, rank : rank + state_dim]
    query_rows = proj_vals[:, rank + state_dim :]
    beta_vals = jax.nn.sigmoid(rows_dot(dt_low, dt_proj) + dt_bias.astype(jnp.float32))
    key_square = jnp.sum(key_rows * key_rows, axis=1, keepdims=True)
    denom_inv = 1.0 / (1.0 + beta_vals * key_square)
    step_rate = beta_vals * denom_inv

    def blocked(values):
        return values.reshape((count_blocks, block_len) + values.shape[1:])

    pieces = (
        blocked(step_rate),
        blocked(conv_vals),
        blocked(key_rows),
        blocked(query_rows),
        blocked(keep_rows),
    )
    unit_state = jnp.ones((width, state_dim), jnp.float32)
    zero_state = jnp.zeros((width, state_dim), jnp.float32)
    total_decay, local_state = lax.scan(block_product, (unit_state, zero_state), pieces)[0]
    state_in = carried_in(
        (total_decay, local_state), "shard", chain_combine, (unit_state, zero_state)
    )[1]
    starts, rec_blocks = lax.scan(block_record, state_in, pieces)[1]
    recurrent = rec_blocks.reshape(tok_local, width)
    skip_vals = d_skip.astype(jnp.float32)
    y_total = recurrent + skip_vals * conv_vals
    gate_act = jax.nn.silu(z_vals)
    gated = (y_total * gate_act).astype(jnp.bfloat16)
    out_val = (x_vals + rows_dot(gated, out_proj)).astype(jnp.bfloat16)
    grad_out_proj = inner_dot(gated, cot_rows)
    grad_gated = outer_dot(cot_rows, out_proj)
    grad_y = grad_gated * gate_act
    grad_z = grad_gated * y_total * silu_slope(z_vals)
    grad_d_skip = jnp.sum(grad_y * conv_vals, axis=0)
    dout_blocks = blocked(grad_y)
    adj_pieces = (pieces[0], pieces[2], pieces[3], pieces[4], dout_blocks)
    grad_local = lax.scan(block_adjoint, zero_state, adj_pieces, reverse=True)[0]
    grad_end = entering(
        (total_decay, grad_local), "shard", chain_combine, (unit_state, zero_state)
    )[1]
    back_pieces = (starts,) + pieces + (dout_blocks,)
    rate_back, conv_back, key_back, query_back = lax.scan(
        block_backward, grad_end, back_pieces, reverse=True
    )[1]
    grad_rate = rate_back.reshape(tok_local, width)
    grad_keys = key_back.reshape(tok_local, state_dim)
    grad_queries = query_back.reshape(tok_local, state_dim)
    grad_conv = grad_y * skip_vals + conv_back.reshape(tok_local, width)
    grad_keys = grad_keys - 2.0 * key_rows * jnp.sum(
        grad_rate * step_rate * step_rate, axis=1, keepdims=True
    )
    grad_dt = grad_rate * denom_inv * denom_inv * beta_vals * (1.0 - beta_vals)
    grad_dt_bias = jnp.sum(grad_dt, axis=0)
    grad_dt_low = grad_dt.astype(jnp.bfloat16)
    grad_dt_proj = inner_dot(dt_low, grad_dt_low)
    grad_dt_in = outer_dot(grad_dt_low, dt_proj)
    grad_proj = jnp.concatenate([grad_dt_in, grad_keys, grad_queries], axis=1).astype(jnp.bfloat16)
    grad_x_proj = inner_dot(grad_proj, conv_out)
    grad_conv = grad_conv + rows_dot(grad_proj, x_proj)
    grad_pre = grad_conv * silu_slope(conv_pre)

    def conv_local(ext_vals, tap_wts, bias_vals):
        return conv_apply(ext_vals, tap_wts, bias_vals, tap_masks)

    conv_pull = jax.vjp(conv_local, extended, conv_w, conv_b)[1]
    grad_ext, grad_conv_weight, grad_conv_bias = conv_pull(grad_pre)
    back_rows = passed_along(grad_ext[: KW - 1].astype(jnp.bfloat16), "shard", -1).astype(
        jnp.float32
    )
    grad_x_part = jnp.concatenate(
        [grad_ext[KW - 1 : tok_local], grad_ext[tok_local:] + back_rows], axis=0
    )
    grad_mixed = jnp.concatenate([grad_x_part, grad_z], axis=1).astype(jnp.bfloat16)
    grad_w_in = inner_dot(normed, grad_mixed)
    grad_normed = outer_dot(grad_mixed, w_in)
    grad_norm_gain = jnp.sum(grad_normed * x_vals * inv_rms, axis=0)
    scaled = grad_normed * gain_vals
    grad_x = inv_rms * (
        scaled - x_vals * inv_rms * inv_rms * jnp.mean(scaled * x_vals, axis=1, keepdims=True)
    )
    dx_val = (cot_rows.astype(jnp.float32) + grad_x).astype(jnp.bfloat16)
    grad_list = (
        grad_norm_gain,
        grad_w_in,
        grad_conv_weight,
        grad_conv_bias,
        grad_x_proj,
        grad_dt_proj,
        grad_dt_bias,
        grad_d_skip,
        grad_out_proj,
    )
    return (out_val, dx_val, grad_list)


def body(
    block_input,
    segment_ids,
    norm_gain,
    w_in,
    conv_weight,
    conv_bias,
    x_proj,
    dt_proj,
    dt_bias,
    d_skip,
    out_proj,
    out_grad,
):
    micro_count = block_input.shape[0]
    tok_local = block_input.shape[1]
    shard_pos = lax.axis_index("shard")
    seg_padded = jnp.pad(segment_ids, ((0, 0), (KW - 1, 0)), constant_values=-1)
    seg_windows = lax.dynamic_slice_in_dim(seg_padded, shard_pos * tok_local, tok_local + KW - 1, 1)
    full_sums = None
    shard_sums = None
    out_rows = []
    grad_rows = []
    for m in range(micro_count):
        gathered = (
            lax.all_gather(norm_gain, "shard", axis=0, tiled=True),
            lax.all_gather(w_in, "shard", axis=1, tiled=True),
            lax.all_gather(conv_weight, "shard", axis=1, tiled=True),
            lax.all_gather(conv_bias, "shard", axis=0, tiled=True),
            lax.all_gather(x_proj, "shard", axis=1, tiled=True),
            lax.all_gather(dt_proj, "shard", axis=1, tiled=True),
            lax.all_gather(dt_bias, "shard", axis=0, tiled=True),
            lax.all_gather(d_skip, "shard", axis=0, tiled=True),
            lax.all_gather(out_proj, "shard", axis=1, tiled=True),
        )
        out_val, dx_val, grad_list = one_batch(
            gathered, block_input[m], out_grad[m], seg_windows[m]
        )
        out_rows.append(out_val)
        grad_rows.append(dx_val)
        full_sums = (
            grad_list if full_sums is None else tuple((a + b for a, b in zip(full_sums, grad_list)))
        )
    shard_sums = (
        lax.psum_scatter(
            full_sums[0].astype(jnp.bfloat16), "shard", scatter_dimension=0, tiled=True
        ).astype(jnp.float32),
        lax.psum_scatter(
            full_sums[1].astype(jnp.bfloat16), "shard", scatter_dimension=1, tiled=True
        ).astype(jnp.float32),
        lax.psum_scatter(
            full_sums[2].astype(jnp.bfloat16), "shard", scatter_dimension=1, tiled=True
        ).astype(jnp.float32),
        lax.psum_scatter(
            full_sums[3].astype(jnp.bfloat16), "shard", scatter_dimension=0, tiled=True
        ).astype(jnp.float32),
        lax.psum_scatter(
            full_sums[4].astype(jnp.bfloat16), "shard", scatter_dimension=1, tiled=True
        ).astype(jnp.float32),
        lax.psum_scatter(
            full_sums[5].astype(jnp.bfloat16), "shard", scatter_dimension=1, tiled=True
        ).astype(jnp.float32),
        lax.psum_scatter(
            full_sums[6].astype(jnp.bfloat16), "shard", scatter_dimension=0, tiled=True
        ).astype(jnp.float32),
        lax.psum_scatter(
            full_sums[7].astype(jnp.bfloat16), "shard", scatter_dimension=0, tiled=True
        ).astype(jnp.float32),
        lax.psum_scatter(
            full_sums[8].astype(jnp.bfloat16), "shard", scatter_dimension=1, tiled=True
        ).astype(jnp.float32),
    )
    large_sums = (
        lax.psum_scatter(shard_sums[1], "replica", scatter_dimension=0, tiled=True),
        lax.psum_scatter(shard_sums[8], "replica", scatter_dimension=0, tiled=True),
    )
    small_sums = lax.psum(
        (
            shard_sums[0],
            shard_sums[2],
            shard_sums[3],
            shard_sums[4],
            shard_sums[5],
            shard_sums[6],
            shard_sums[7],
        ),
        "replica",
    )
    return (
        jnp.stack(out_rows),
        jnp.stack(grad_rows),
        small_sums[0],
        large_sums[0],
        small_sums[1],
        small_sums[2],
        small_sums[3],
        small_sums[4],
        small_sums[5],
        small_sums[6],
        large_sums[1],
    )


def solution(mesh):
    return jax.shard_map(
        body,
        mesh=mesh,
        in_specs=(
            P("replica", "shard", None),
            P("replica", None),
            P("shard"),
            P(None, "shard"),
            P(None, "shard"),
            P("shard"),
            P(None, "shard"),
            P(None, "shard"),
            P("shard"),
            P("shard"),
            P(None, "shard"),
            P("replica", "shard", None),
        ),
        out_specs=(
            P("replica", "shard", None),
            P("replica", "shard", None),
            P("shard"),
            P("replica", "shard"),
            P(None, "shard"),
            P("shard"),
            P(None, "shard"),
            P(None, "shard"),
            P("shard"),
            P("shard"),
            P("replica", "shard"),
        ),
        check_vma=False,
    )
```

profile of v0, /device:TPU:0, one launch (start us, length us, event | category | flops | bytes accessed | tf_op | source)
XLA Modules:
  0.0 2360.5 jit_solution(17861980219472843263)
XLA Ops:
  42.2 171.9 %all-gather.18.cloned.1.call-done = bf16[2048,8192]{1,0:T(8,128)(2,1)} async-done(((bf16[2048,2048]{1,0:T(8,128)(2,1)}), bf16[2048,8192]{1,0:T(8,128)(2,1)}) %all-gather.18.cloned.1.call-update) | async-done | bytes 33554448 | tf_op jit(solution)/shard_map/all_gather | solution.py:289
  214.1 15.5 convolution_convert_fusion.1
  231.8 14.6 convolution_convert_fusion
  252.0 69.6 %all-gather.24.cloned.1.call-done = bf16[4096,2048]{1,0:T(8,128)(2,1)} async-done(((bf16[4096,512]{1,0:T(8,128)(2,1)}), bf16[4096,2048]{1,0:T(8,128)(2,1)}) %all-gather.24.cloned.1.call-update) | async-done | bytes 16777232 | tf_op jit(solution)/shard_map/all_gather | solution.py:296
  321.6 15.2 multiply_reduce_fusion.193
  345.4 14.9 all-gather.22.cloned.1.call-done
  363.1 102.7 %while.190 = (s32[]{:T(128)}, f32[4096,16]{0,1:T(8,128)S(1)}, f32[4096,16]{0,1:T(8,128)}, f32[4,16,4096]{2,1,0:T(8,128)S(1)}, f32[4,16,16]{2,1,0:T(8,128)}, /*in...) while((s32[]{:T(128)}, f32[4096,16]{0,1:T(8,128)S(1)}, ...), condition=%wide.region_3.4_spmd.clone, body=%wide.region_2.3_spmd.clone.sunk | while | flops 10682642 | bytes 5774296 | solution.py:186
  366.7 11.3 multiply_add_fusion.148
  468.5 15.7 multiply_reduce_fusion.192
  489.1 102.7 %while.192 = (s32[]{:T(128)}, f32[4096,16]{0,1:T(8,128)S(1)}, f32[4096,16]{0,1:T(8,128)S(1)}, f32[4,16,4096]{2,1,0:T(8,128)S(1)}, f32[4,16,16]{2,1,0:T(8,128)S(1...) while((s32[]{:T(128)}, f32[4096,16]{0,1:T(8,128)S(1)}, ...), condition=%wide.region_27.28_spmd.clone, body=%wide.region_26.27_spmd.clone.sunk | while | flops 10682642 | bytes 3677088 | solution.py:186
  592.6 65.8 %while.194 = (s32[]{:T(128)}, f32[4096,16]{0,1:T(8,128)S(1)}, f32[4,16,4096]{2,1,0:T(8,128)S(1)}, f32[4,16,16]{2,1,0:T(8,128)}, f32[4,16]{1,0:T(4,128)}, /*index...) while((s32[]{:T(128)}, f32[4096,16]{0,1:T(8,128)S(1)}, ...), condition=%wide.region_49.50_spmd.clone, body=%wide.region_48.49_spmd.clone.sunk | while | flops 6357267 | bytes 2104179 | solution.py:204
  679.0 60.7 %while.195 = (s32[]{:T(128)}, f32[4096,16]{0,1:T(8,128)S(1)}, f32[4,16,4096]{2,1,0:T(8,128)S(1)}, f32[4,16,16]{2,1,0:T(8,128)S(1)}, f32[4,16]{1,0:T(4,128)S(1)},...) while((s32[]{:T(128)}, f32[4096,16]{0,1:T(8,128)S(1)}, ...), condition=%wide.region_137.138_spmd.clone, body=%wide.region_136.137_spmd.clone.sunk | while | flops 6357267 | bytes 2104179 | solution.py:204
  682.6 11.4 add_multiply_fusion.5
  698.1 11.4 add_multiply_fusion.5
  713.2 11.4 add_multiply_fusion.5
  728.2 11.4 add_multiply_fusion.5
  774.1 119.0 %while.184 = (s32[]{:T(128)}, f32[4096,16]{0,1:T(8,128)S(1)}, f32[4,4096,16]{1,2,0:T(8,128)}, f32[4,16,4096]{2,1,0:T(8,128)}, f32[4,16,4096]{2,1,0:T(8,128)S(1)}...) while((s32[]{:T(128)}, f32[4096,16]{0,1:T(8,128)S(1)}, ...), condition=%wide.region_23.24_spmd, body=%wide.region_6.23_spmd.sunk | while | flops 11534609 | bytes 8923085 | solution.py:190
  782.2 11.6 multiply_reduce_fusion.240
  811.8 11.6 multiply_reduce_fusion.240
  841.5 11.6 multiply_reduce_fusion.240
  871.4 11.6 multiply_reduce_fusion.240
  895.3 203.1 %while.187 = (s32[]{:T(128)}, f32[4096,16]{0,1:T(8,128)S(1)}, f32[4,16,4096]{2,1,0:T(8,128)}, f32[4,16,4096]{2,1,0:T(8,128)}, f32[4,16,16]{2,1,0:T(8,128)S(1)}, ...) while((s32[]{:T(128)}, f32[4096,16]{0,1:T(8,128)S(1)}, ...), condition=%wide.region_133.134_spmd, body=%wide.region_52.133_spmd.sunk | while | flops 34942480 | bytes 17066536 | solution.py:209
  903.1 11.3 multiply_add_fusion.146
  953.7 11.3 multiply_add_fusion.146
  1004.6 11.3 multiply_add_fusion.146
  1055.1 11.3 multiply_add_fusion.146
  1113.8 98.0 %while.185 = (s32[]{:T(128)}, f32[4096,16]{0,1:T(8,128)S(1)}, f32[4,4096,16]{1,2,0:T(8,128)}, f32[4,16,4096]{2,1,0:T(8,128)}, f32[4,16,4096]{2,1,0:T(8,128)S(1)}...) while((s32[]{:T(128)}, f32[4096,16]{0,1:T(8,128)S(1)}, ...), condition=%wide.region_47.48_spmd, body=%wide.region_30.47_spmd.sunk | while | flops 11534609 | bytes 8923085 | solution.py:190
  1119.4 12.0 multiply_reduce_fusion.249
  1143.9 12.0 multiply_reduce_fusion.249
  1168.4 12.0 multiply_reduce_fusion.249
  1192.7 12.0 multiply_reduce_fusion.249
  1213.9 195.1 %while.189 = (s32[]{:T(128)}, f32[4096,16]{0,1:T(8,128)S(1)}, f32[4,16,4096]{2,1,0:T(8,128)}, f32[4,16,4096]{2,1,0:T(8,128)}, f32[4,16,16]{2,1,0:T(8,128)S(1)}, ...) while((s32[]{:T(128)}, f32[4096,16]{0,1:T(8,128)S(1)}, ...), condition=%wide.region_221.222_spmd, body=%wide.region_140.221_spmd.sunk | while | flops 34942480 | bytes 17066536 | solution.py:209
  1218.9 11.7 multiply_add_fusion.147
  1268.0 11.7 multiply_add_fusion.147
  1316.7 11.7 multiply_add_fusion.147
  1365.4 11.7 multiply_add_fusion.147
  1415.6 13.6 fusion.432
  1429.1 18.9 add_convert_fusion.1
  1465.5 26.1 %fusion.425 = f32[2048,8192]{1,0:T(8,128)} fusion(bf16[64,4096]{1,0:T(8,128)(2,1)S(1)} %copy-done.18, bf16[3,4096]{1,0:T(4,128)(2,1)S(1)} %fusion.446, bf16[61,4096]{1,0:T(8,128)(2,1)S(1)} %slice.5298, f32[2048]{0:T(1024)S(1)} %bitcast.3490, f32[64]{0:T(128)S(1)} %copy-done.54, bf16[2,64,2048]{2,1,0:T(8,128)(2,1)S(1)} %copy-done.2), kind=kOutput, calls=%fused_computation.1561 | convolution fusion | flops 2151153664 | bytes 68461056 | tf_op jit(solution)/shard_map/dot_general | solution.py:59
  1491.6 33.7 %add_convert_fusion = bf16[2048,8192]{1,0:T(8,128)(2,1)} fusion(f32[2048,8192]{1,0:T(8,128)} %fusion.425, bf16[64,4096]{1,0:T(8,128)(2,1)S(1)} %copy-done.19, bf16[3,4096]{1,0:T(4,128)(2,1)S(1)} %fusion.445, bf16[61,4096]{1,0:T(8,128)(2,1)} %slice.5301, f32[64]{0:T(128)S(1)} %copy-done.52, f32[2048]{0:T(1024)S(1)} %bitcast.3491, ...), kind=kOutput, calls=%fused_computation.1428 | convolution fusion | flops 2184708096 | bytes 101990912 | tf_op jit(solution)/shard_map/dot_general | solution.py:59
  1536.4 38.0 %reduce-scatter.18.cloned.1.call-done = bf16[4096,512]{1,0:T(8,128)(2,1)} async-done(((bf16[4096,2048]{1,0:T(8,128)(2,1)}), bf16[4096,512]{1,0:T(8,128)(2,1)}) %reduce-scatter.18.cloned.1.call-update) | async-done | bytes 4194320 | tf_op jit(solution)/shard_map/reduce_scatter | solution.py:331
  1581.3 230.6 %reduce-scatter.10.cloned.1.call-done = bf16[2048,2048]{1,0:T(8,128)(2,1)} async-done(((bf16[2048,8192]{1,0:T(8,128)(2,1)}), bf16[2048,2048]{1,0:T(8,128)(2,1)}) %reduce-scatter.10.cloned.1.call-update) | async-done | bytes 8388624 | tf_op jit(solution)/shard_map/reduce_scatter | solution.py:310
  1811.9 11.6 convert_element_type.346
  1845.0 15.8 fusion.424
  1860.8 15.9 fusion.419
  1896.1 98.4 %all-reduce.216 = (f32[512]{0:T(512)}, f32[4,1024]{1,0:T(4,128)}, f32[1024]{0:T(1024)}, f32[160,1024]{1,0:T(8,128)}, f32[128,1024]{1,0:T(8,128)}, /*index=5*/f32[1024]{0:T(1024)}, f32[1024]{0:T(1024)}) all-reduce(f32[512]{0:T(512)S(1)} %dynamic-slice_convert_fusion.3, ...), channel_id=1, replica_groups=mesh['replica'=8,'shard'=4] {'replica'}, use_global_device_ids=true, to_apply=%region_227.228 | all-reduce | flops 302592 | bytes 1822720 | tf_op jit(solution)/shard_map/psum | solution.py:339
  1994.5 73.0 %reduce-scatter.20.cloned.1.call-done = f32[512,512]{1,0:T(8,128)} async-done(((f32[4096,512]{1,0:T(8,128)}), f32[512,512]{1,0:T(8,128)}) %reduce-scatter.20.cloned.1.call-update) | async-done | bytes 1048592 | tf_op jit(solution)/shard_map/reduce_scatter | solution.py:337
  2067.5 286.3 %reduce-scatter.12.cloned.1.call-done = f32[256,2048]{1,0:T(8,128)} async-done(((f32[2048,2048]{1,0:T(8,128)}), f32[256,2048]{1,0:T(8,128)}) %reduce-scatter.12.cloned.1.call-update) | async-done | bytes 2097168 | tf_op jit(solution)/shard_map/reduce_scatter | solution.py:336
  (1389 shorter events, 934.8 us)
Async XLA Ops:
  7.2 206.9 %all-gather.18.cloned.1.call-start = ((), (), s32[]{:S(2)}) async-start(), calls=%async_computation.7 | async-start | bytes 41943040 | tf_op jit(solution)/shard_map/all_gather | solution.py:289
  8.0 17.4 copy-start.76
  8.0 22.5 copy-start.77
  8.0 28.3 %copy-start.71 = (bf16[4,1024]{1,0:T(4,128)(2,1)S(1)}, bf16[4,1024]{1,0:T(4,128)(2,1)}, u32[]{:S(2)}) copy-start(bf16[4,1024]{1,0:T(4,128)(2,1)} %param.40) | copy-start | bytes 24580
  8.0 313.6 %all-gather.24.cloned.1.call-start = ((), (), s32[]{:S(2)}) async-start(), calls=%async_computation.10 | async-start | bytes 20971520 | tf_op jit(solution)/shard_map/all_gather | solution.py:296
  8.7 333.4 %all-gather.20.cloned.1.call-start = ((), (), s32[]{:S(2)}) async-start(), calls=%async_computation.8 | async-start | bytes 1638400 | tf_op jit(solution)/shard_map/all_gather | solution.py:292
  9.5 350.8 %all-gather.22.cloned.1.call-start = ((), (), s32[]{:S(2)}) async-start(), calls=%async_computation.9 | async-start | bytes 1310720 | tf_op jit(solution)/shard_map/all_gather | solution.py:293
  10.0 748.7 %all-gather.28.cloned.1.call-start = ((), (), s32[]{:S(2)}) async-start(), calls=%async_computation.18 | async-start | bytes 1310720 | tf_op jit(solution)/shard_map/all_gather | solution.py:19
  11.8 217.8 %copy-start.53 = (f32[64]{0:T(128)}, f32[64]{0:T(128)S(1)}, u32[]{:S(2)}) copy-start(f32[64]{0:T(128)S(1)} %add_rsqrt_fusion.1) | copy-start | bytes 772
  11.8 220.0 %copy-start.51 = (f32[64]{0:T(128)}, f32[64]{0:T(128)S(1)}, u32[]{:S(2)}) copy-start(f32[64]{0:T(128)S(1)} %add_rsqrt_fusion) | copy-start | bytes 772
  19.3 212.5 %copy-start.33 = (f32[4,1,512]{2,1,0:T(1,128)}, f32[4,1,512]{2,1,0:T(1,128)S(1)}, u32[]{:S(2)}) copy-start(f32[4,1,512]{2,1,0:T(1,128)S(1)} %convert_element_type.375) | copy-start | bytes 24580
  229.6 92.0 %copy-start.26 = (bf16[64,8192]{1,0:T(8,128)(2,1)}, bf16[64,8192]{1,0:T(8,128)(2,1)S(1)}, u32[]{:S(2)}) copy-start(bf16[64,8192]{1,0:T(8,128)(2,1)S(1)} %convolution_convert_fusion.1) | copy-start | bytes 3145732
  229.7 21.2 collective-permute-start
  246.5 75.2 %copy-start.30 = (bf16[2,64,2048]{2,1,0:T(8,128)(2,1)S(1)}, bf16[2,64,2048]{2,1,0:T(8,128)(2,1)}, u32[]{:S(2)}) copy-start(bf16[2,64,2048]{2,1,0:T(8,128)(2,1)} %param.47) | copy-start | bytes 1572868
  248.4 217.7 %collective-permute-start.1 = (bf16[3,4096]{1,0:T(4,128)(2,1)S(1)}, bf16[3,4096]{1,0:T(4,128)(2,1)S(1)}, u32[]{:S(2)}, u32[]{:S(2)}) collective-permute-start(bf16[3,4096]{1,0:T(4,128)(2,1)S(1)} %slice.5288), channel_id=1, source_target_pairs={{0,1},{1,2},{2,3},{4,5},{5,6},{6,7},{8,9},{9,10},{10,11},{12,13},{... | collective-permute-start | bytes 73736 | tf_op jit(solution)/shard_map/ppermute | solution.py:14
  336.9 23.4 copy-start.11
  344.0 19.1 copy-start.45
  363.1 105.4 %copy-start.59 = (f32[4096]{0:T(1024)S(1)}, f32[4096]{0:T(1024)}, u32[]{:S(2)}) copy-start(f32[4096]{0:T(1024)} %convert_element_type.292) | copy-start | bytes 49156
  363.1 105.4 %copy-start.64 = (f32[1,4096]{1,0:T(1,128)S(1)}, f32[1,4096]{1,0:T(1,128)}, u32[]{:S(2)}) copy-start(f32[1,4096]{1,0:T(1,128)} %get-tuple-element.3206) | copy-start | bytes 49156
  363.1 105.4 %copy-start.66 = (f32[1,4096]{1,0:T(1,128)S(1)}, f32[1,4096]{1,0:T(1,128)}, u32[]{:S(2)}) copy-start(f32[1,4096]{1,0:T(1,128)} %get-tuple-element.3207) | copy-start | bytes 49156
  363.1 105.4 %copy-start.68 = (f32[1,4096]{1,0:T(1,128)S(1)}, f32[1,4096]{1,0:T(1,128)}, u32[]{:S(2)}) copy-start(f32[1,4096]{1,0:T(1,128)} %get-tuple-element.3208) | copy-start | bytes 49156
  465.8 18.4 copy-start
  465.8 18.3 copy-start.4
  465.8 295.8 %all-gather.26.cloned.1.call-start = ((), (), s32[]{:S(2)}) async-start(), calls=%async_computation.17 | async-start | bytes 1310720 | tf_op jit(solution)/shard_map/all_gather | solution.py:19
  591.9 86.1 %copy-start.3 = (f32[4096,16]{0,1:T(8,128)}, f32[4096,16]{0,1:T(8,128)S(1)}, u32[]{:S(2)}) copy-start(f32[4096,16]{0,1:T(8,128)S(1)} %get-tuple-element.1341) | copy-start | bytes 786436
  591.9 506.5 %all-gather.32.cloned.1.call-start = ((), (), s32[]{:S(2)}) async-start(), calls=%async_computation.20 | async-start | bytes 1310720 | tf_op jit(solution)/shard_map/all_gather | solution.py:19
  592.6 65.8 %copy-start.5 = (f32[4096,16]{0,1:T(8,128)S(1)}, f32[4096,16]{0,1:T(8,128)}, u32[]{:S(2)}) copy-start(f32[4096,16]{0,1:T(8,128)} %copy-done.4) | copy-start | bytes 786436
  674.6 426.8 %all-gather.30.cloned.1.call-start = ((), (), s32[]{:S(2)}) async-start(), calls=%async_computation.19 | async-start | bytes 1310720 | tf_op jit(solution)/shard_map/all_gather | solution.py:19
  678.7 895.7 %reduce-scatter.18.cloned.1.call-start = ((), (), s32[]{:S(2)}) async-start(), calls=%async_computation.15 | async-start | bytes 20971520 | tf_op jit(solution)/shard_map/reduce_scatter | solution.py:331
  739.6 15.7 copy-start.35
  739.7 15.7 copy-start.41
  739.7 15.7 copy-start.80
  1213.9 195.1 %copy-start.12 = (bf16[64,4096]{1,0:T(8,128)(2,1)S(1)}, bf16[64,4096]{1,0:T(8,128)(2,1)}, u32[]{:S(2)}) copy-start(bf16[64,4096]{1,0:T(8,128)(2,1)} %copy-done.11) | copy-start | bytes 1572868
  1213.9 195.1 %copy-start.50 = (f32[4096]{0:T(1024)S(1)}, f32[4096]{0:T(1024)}, u32[]{:S(2)}) copy-start(f32[4096]{0:T(1024)} %convert_element_type.309) | copy-start | bytes 49156
  1415.6 13.6 copy-start.15
  1448.1 363.8 %reduce-scatter.10.cloned.1.call-start = ((), (), s32[]{:S(2)}) async-start(), calls=%async_computation.11 | async-start | bytes 41943040 | tf_op jit(solution)/shard_map/reduce_scatter | solution.py:310
  1455.7 7.4 collective-permute-start.2
  1460.9 30.8 %copy-start.20 = (bf16[61,4096]{1,0:T(8,128)(2,1)}, bf16[61,4096]{1,0:T(8,128)(2,1)S(1)}, u32[]{:S(2)}) copy-start(bf16[61,4096]{1,0:T(8,128)(2,1)S(1)} %slice.5298) | copy-start | bytes 1499140
  1461.8 3.6 collective-permute-start.3
  1465.5 26.1 %copy-start.19 = (bf16[64,4096]{1,0:T(8,128)(2,1)S(1)}, bf16[64,4096]{1,0:T(8,128)(2,1)}, u32[]{:S(2)}) copy-start(bf16[64,4096]{1,0:T(8,128)(2,1)} %get-tuple-element.3213) | copy-start | bytes 1572868
  1465.5 26.1 %copy-start.52 = (f32[64]{0:T(128)S(1)}, f32[64]{0:T(128)}, u32[]{:S(2)}) copy-start(f32[64]{0:T(128)} %copy-done.51) | copy-start | bytes 772
  1525.4 363.1 %reduce-scatter.22.cloned.1.call-start = ((), (), s32[]{:S(2)}) async-start(), calls=%async_computation.21 | async-start | bytes 1310720
  1530.6 359.0 %reduce-scatter.16.cloned.1.call-start = ((), (), s32[]{:S(2)}) async-start(), calls=%async_computation.14 | async-start | bytes 1310720 | tf_op jit(solution)/shard_map/reduce_scatter | solution.py:322
  1533.7 362.4 %reduce-scatter.14.cloned.1.call-start = ((), (), s32[]{:S(2)}) async-start(), calls=%async_computation.13 | async-start | bytes 1638400 | tf_op jit(solution)/shard_map/reduce_scatter | solution.py:319
  1536.4 531.2 %reduce-scatter.20.cloned.1.call-start = ((), (), s32[]{:S(2)}) async-start(), calls=%async_computation.16 | async-start | bytes 9437184 | tf_op jit(solution)/shard_map/reduce_scatter | solution.py:337
  1581.1 772.8 %reduce-scatter.12.cloned.1.call-start = ((), (), s32[]{:S(2)}) async-start(), calls=%async_computation.12 | async-start | bytes 18874368 | tf_op jit(solution)/shard_map/reduce_scatter | solution.py:336
  1845.0 15.8 copy-start.21
  1860.8 26.4 %copy-start.32 = (bf16[2,64,2048]{2,1,0:T(8,128)(2,1)S(1)}, bf16[2,64,2048]{2,1,0:T(8,128)(2,1)}, u32[]{:S(2)}) copy-start(bf16[2,64,2048]{2,1,0:T(8,128)(2,1)} %param.47) | copy-start | bytes 1572868
  (69 other events, 255.5 us)
Sparse Core Ops, SparseCore 0:
  9.6 204.4 all-gather.17
  215.7 105.9 all-gather.23
  323.2 18.8 all-gather.19
  343.5 16.7 all-gather.21
  466.0 16.7 all-gather.27
  592.0 16.7 all-gather.25
  674.7 16.7 all-gather.31
  693.1 16.7 all-gather.29
  1448.2 126.1 reduce-scatter.17
  1577.0 234.8 reduce-scatter.9
  1814.6 24.8 reduce-scatter.21
  1841.9 24.8 reduce-scatter.15
  1869.5 26.5 reduce-scatter.13
  1900.2 167.2 reduce-scatter.19
  2072.2 281.5 reduce-scatter.11
where the time goes:
time: 2380 us; the launch traced here: 2360 us
  waiting for transfers between devices  901 us (38%)
  other arithmetic  841 us (35%)
  matrix products  225 us (9%)
  local copies, waits for them, and re-layouts  197 us (8%)
  blocking collectives  164 us (7%)
    reduce_scatter x1, waiting for transfers between devices, body(): lax.psum_scatter(shard_sums[1], 'replica', scatter_dimension=0, tiled=True)  286 us
    reduce_scatter x1, waiting for transfers between devices, body(): lax.psum_scatter(full_sums[1].astype(jnp.bfloat16), 'shard', scatter_dime...  231 us
    reduce_sum x72, other arithmetic, decay_of(): return (1.0 - rate_row[:, None] * (key_row * key_row)[None, :]) * keep_val  219 us
    all_gather x1, waiting for transfers between devices, body(): lax.all_gather(w_in, 'shard', axis=1, tiled=True)  172 us
    reduce_sum x72, other arithmetic, block_forward(): outputs.append(jnp.sum(carried * query_blk[t][None, :], axis=1))  157 us
    dot_general x8, matrix products, inner_dot(): lax.dot_general(first_op, second_op, (((0,), (0,)), ((), ())), preferred_...  100 us
    psum x1, blocking collectives, body(): lax.psum((shard_sums[0], shard_sums[2], shard_sums[3], shard_sums[4], sha...  98.4 us
    add x8, other arithmetic, block_forward(): decay_now * carried  92.3 us
  transfers between devices with their start and end apart: 19, of which 10 were waited for; matrix products, arithmetic and copies ran while one was open for 39% of the time, Pallas kernels for 0%

commit v1 on v0

--- a/solution.py
+++ b/solution.py
@@ -6,6 +6,24 @@
 KW = 4
 EPS = 1e-05
 block_len = 16
+
+
+def ring_gather(array, axis, dim):
+    ways, here, lap = (lax.axis_size(axis), lax.axis_index(axis), array.shape[dim])
+    shape = [n * ways if d == dim else n for d, n in enumerate(array.shape)]
+    full = lax.dynamic_update_slice_in_dim(
+        jnp.zeros(shape, array.dtype), array, here * lap, axis=dim
+    )
+    going_up = going_down = array
+    for far in range(1, ways // 2 + 1):
+        going_up = lax.ppermute(going_up, axis, [(d, (d + 1) % ways) for d in range(ways)])
+        full = lax.dynamic_update_slice_in_dim(full, going_up, (here - far) % ways * lap, axis=dim)
+        if 2 * far < ways:
+            going_down = lax.ppermute(going_down, axis, [(d, (d - 1) % ways) for d in range(ways)])
+            full = lax.dynamic_update_slice_in_dim(
+                full, going_down, (here + far) % ways * lap, axis=dim
+            )
+    return full
 
 
 def passed_along(block, axis, distance):
@@ -286,7 +304,7 @@
     for m in range(micro_count):
         gathered = (
             lax.all_gather(norm_gain, "shard", axis=0, tiled=True),
-            lax.all_gather(w_in, "shard", axis=1, tiled=True),
+            ring_gather(w_in, "shard", 1),
             lax.all_gather(conv_weight, "shard", axis=1, tiled=True),
             lax.all_gather(conv_bias, "shard", axis=0, tiled=True),
             lax.all_gather(x_proj, "shard", axis=1, tiled=True),

time: 2380 us -> 2700 us (1.13)
  other arithmetic: 841 us -> 966 us
  blocking collectives: 164 us -> 265 us
  local copies, waits for them, and re-layouts: 197 us -> 266 us
    ppermute x0 -> x3, waiting for transfers between devices: none -> 268 us  [the longest x2 268 us: ring_gather(): lax.ppermute(going_up, axis, [(d, (d + 1) % ways) for d in range(ways)])]
    all_gather x1 -> x0, waiting for transfers between devices: 172 us -> none  [body(): lax.all_gather(w_in, 'shard', axis=1, tiled=True)]
    all_gather x1, blocking collectives: 6.11 us -> 103 us  [body(): lax.all_gather(norm_gain, 'shard', axis=0, tiled=True)]
    mul x128, other arithmetic: 0.74 us -> 93.2 us  [block_product(): rate_blk[t] * conv_blk[t]]
    all_gather x1, waiting for transfers between devices: 69.6 us -> 0.01 us  [body(): lax.all_gather(out_proj, 'shard', axis=1, tiled=True)]
    dynamic_update_slice x0 -> x4, local copies, waits for them, and re-layouts: none -> 32.9 us  [the longest x2 16.5 us: ring_gather(): lax.dynamic_update_slice_in_dim(full, going_up, (here - far) % ways * lap...]
    mul x32, other arithmetic: 20.4 us -> 48.3 us  [decay_of(): return (1.0 - rate_row[:, None] * (key_row * key_row)[None, :]) * keep_val]
  transfers between devices with their start and end apart: 19 -> 21, of which waited for: 10 -> 7; matrix products, arithmetic and copies ran while one was open for 39% -> 35% of each run, Pallas kernels for 0% -> 0%
where the time goes in v1:
time: 2700 us; the launch traced here: 2670 us
  other arithmetic  966 us (36%)
  waiting for transfers between devices  909 us (34%)
  local copies, waits for them, and re-layouts  266 us (10%)
  blocking collectives  265 us (10%)
  matrix products  221 us (8%)
    reduce_scatter x1, waiting for transfers between devices, body(): lax.psum_scatter(shard_sums[1], 'replica', scatter_dimension=0, tiled=True)  286 us
    ppermute x2, waiting for transfers between devices, ring_gather(): lax.ppermute(going_up, axis, [(d, (d + 1) % ways) for d in range(ways)])  268 us
    reduce_scatter x1, waiting for transfers between devices, body(): lax.psum_scatter(full_sums[1].astype(jnp.bfloat16), 'shard', scatter_dime...  231 us
    reduce_sum x72, other arithmetic, decay_of(): return (1.0 - rate_row[:, None] * (key_row * key_row)[None, :]) * keep_val  209 us
    reduce_sum x72, other arithmetic, block_forward(): outputs.append(jnp.sum(carried * query_blk[t][None, :], axis=1))  157 us
    all_gather x1, blocking collectives, body(): lax.all_gather(norm_gain, 'shard', axis=0, tiled=True)  103 us
    psum x1, blocking collectives, body(): lax.psum((shard_sums[0], shard_sums[2], shard_sums[3], shard_sums[4], sha...  98.9 us
    add x8, other arithmetic, block_product(): decay_now * local_state  98.8 us
  transfers between devices with their start and end apart: 21, of which 7 were waited for; matrix products, arithmetic and copies ran while one was open for 35% of the time, Pallas kernels for 0%

profile of v1, /device:TPU:0, one launch (start us, length us, event | category | flops | bytes accessed | tf_op | source)
XLA Modules:
  0.0 2665.4 jit_solution(10485150160712981154)
XLA Ops:
  10.5 268.5 %collective-permute-done = bf16[2048,2048]{1,0:T(8,128)(2,1)} collective-permute-done((bf16[2048,2048]{1,0:T(8,128)(2,1)}, bf16[2048,2048]{1,0:T(8,128)(2,1)}, u32[]{:S(2)}, u32[]{:S(2)}) %collective-permute-start) | collective-permute-done | bytes 8388640 | tf_op jit(solution)/shard_map/ppermute | solution.py:19
  283.1 102.5 %all-gather.8 = bf16[4,1,512]{2,1,0:T(2,128)(2,1)S(1)} all-gather(bf16[1,1,512]{2,1,0:T(2,128)(2,1)S(1)} %reshape.7362), channel_id=1, replica_groups=mesh['replica'=8,'shard'=4] {'shard'}, dimensions={0}, use_global_device_ids=true | all-gather | bytes 5120 | tf_op jit(solution)/shard_map/all_gather | solution.py:306
  456.4 13.8 convolution_convert_fusion.1
  472.5 13.8 convolution_convert_fusion
  493.6 15.2 multiply_reduce_fusion.193
  514.6 160.4 %while.190 = (s32[]{:T(128)}, f32[4096,16]{0,1:T(8,128)S(1)}, f32[4096,16]{0,1:T(8,128)}, f32[4,16,4096]{2,1,0:T(8,128)S(1)}, f32[4,16,16]{2,1,0:T(8,128)}, /*in...) while((s32[]{:T(128)}, f32[4096,16]{0,1:T(8,128)S(1)}, ...), condition=%wide.region_3.4_spmd.clone, body=%wide.region_2.3_spmd.clone.sunk | while | flops 10682642 | bytes 3677088 | solution.py:204
  542.0 12.5 multiply_add_fusion.148
  581.9 12.7 multiply_add_fusion.148
  622.1 12.7 multiply_add_fusion.148
  662.2 12.7 multiply_add_fusion.148
  676.1 77.7 %while.194 = (s32[]{:T(128)}, f32[4096,16]{0,1:T(8,128)}, f32[4,16,4096]{2,1,0:T(8,128)S(1)}, f32[4,16,16]{2,1,0:T(8,128)}, f32[4,16]{1,0:T(4,128)}, /*index=5*/...) while((s32[]{:T(128)}, f32[4096,16]{0,1:T(8,128)}, ...), condition=%wide.region_49.50_spmd.clone, body=%wide.region_48.49_spmd.clone.sunk | while | flops 6357267 | bytes 2104179 | solution.py:222
  682.7 12.6 add_multiply_fusion.4
  701.9 12.8 add_multiply_fusion.4
  721.4 12.8 add_multiply_fusion.4
  741.0 12.8 add_multiply_fusion.4
  753.7 15.4 multiply_reduce_fusion.192
  774.7 167.5 %while.192 = (s32[]{:T(128)}, f32[4096,16]{0,1:T(8,128)S(1)}, f32[4096,16]{0,1:T(8,128)S(1)}, f32[4,16,4096]{2,1,0:T(8,128)S(1)}, f32[4,16,16]{2,1,0:T(8,128)}, ...) while((s32[]{:T(128)}, f32[4096,16]{0,1:T(8,128)S(1)}, ...), condition=%wide.region_27.28_spmd.clone, body=%wide.region_26.27_spmd.clone.sunk | while | flops 10682642 | bytes 3677088 | solution.py:204
  804.5 12.0 multiply_add_fusion.149
  846.3 12.0 multiply_add_fusion.149
  888.1 12.0 multiply_add_fusion.149
  930.2 12.0 multiply_add_fusion.149
  942.9 74.7 %while.195 = (s32[]{:T(128)}, f32[4096,16]{0,1:T(8,128)S(1)}, f32[4,16,4096]{2,1,0:T(8,128)S(1)}, f32[4,16,16]{2,1,0:T(8,128)}, f32[4,16]{1,0:T(4,128)}, /*index...) while((s32[]{:T(128)}, f32[4096,16]{0,1:T(8,128)S(1)}, ...), condition=%wide.region_137.138_spmd.clone, body=%wide.region_136.137_spmd.clone.sunk | while | flops 6357267 | bytes 2104179 | solution.py:222
  949.9 11.9 add_multiply_fusion.5
  968.3 11.9 add_multiply_fusion.5
  987.1 11.9 add_multiply_fusion.5
  1005.7 11.9 add_multiply_fusion.5
  1063.5 12.3 while.191
  1077.9 122.3 %while.184 = (s32[]{:T(128)}, f32[4096,16]{0,1:T(8,128)S(1)}, f32[4,4096,16]{1,2,0:T(8,128)}, f32[4,16,4096]{2,1,0:T(8,128)}, f32[4,16,4096]{2,1,0:T(8,128)S(1)}...) while((s32[]{:T(128)}, f32[4096,16]{0,1:T(8,128)S(1)}, ...), condition=%wide.region_23.24_spmd, body=%wide.region_6.23_spmd.sunk | while | flops 11534609 | bytes 8923085 | solution.py:208
  1086.2 11.7 multiply_reduce_fusion.240
  1147.2 11.7 multiply_reduce_fusion.240
  1202.3 198.0 %while.187 = (s32[]{:T(128)}, f32[4096,16]{0,1:T(8,128)S(1)}, f32[4,16,4096]{2,1,0:T(8,128)}, f32[4,16,4096]{2,1,0:T(8,128)}, f32[4,16,16]{2,1,0:T(8,128)S(1)}, ...) while((s32[]{:T(128)}, f32[4096,16]{0,1:T(8,128)S(1)}, ...), condition=%wide.region_133.134_spmd, body=%wide.region_52.133_spmd.sunk | while | flops 34942480 | bytes 21260876 | solution.py:227
  1415.8 103.9 %while.185 = (s32[]{:T(128)}, f32[4096,16]{0,1:T(8,128)S(1)}, f32[4,4096,16]{1,2,0:T(8,128)}, f32[4,16,4096]{2,1,0:T(8,128)}, f32[4,16,4096]{2,1,0:T(8,128)S(1)}...) while((s32[]{:T(128)}, f32[4096,16]{0,1:T(8,128)S(1)}, ...), condition=%wide.region_47.48_spmd, body=%wide.region_30.47_spmd.sunk | while | flops 11534609 | bytes 8923085 | solution.py:208
  1422.9 11.8 multiply_reduce_fusion.249
  1448.8 11.8 multiply_reduce_fusion.249
  1474.7 11.8 multiply_reduce_fusion.249
  1500.8 11.8 multiply_reduce_fusion.249
  1521.9 191.8 %while.189 = (s32[]{:T(128)}, f32[4096,16]{0,1:T(8,128)S(1)}, f32[4,16,4096]{2,1,0:T(8,128)}, f32[4,16,4096]{2,1,0:T(8,128)}, f32[4,16,16]{2,1,0:T(8,128)S(1)}, ...) while((s32[]{:T(128)}, f32[4096,16]{0,1:T(8,128)S(1)}, ...), condition=%wide.region_221.222_spmd, body=%wide.region_140.221_spmd.sunk | while | flops 34942480 | bytes 21260876 | solution.py:227
  1720.3 13.3 fusion.432
  1733.6 18.9 add_convert_fusion.1
  1769.4 26.4 fusion.425
  1795.8 34.0 %add_convert_fusion = bf16[2048,8192]{1,0:T(8,128)(2,1)} fusion(f32[2048,8192]{1,0:T(8,128)} %fusion.425, bf16[64,4096]{1,0:T(8,128)(2,1)S(1)} %copy-done.24, bf16[3,4096]{1,0:T(4,128)(2,1)S(1)} %fusion.445, bf16[61,4096]{1,0:T(8,128)(2,1)S(1)} %slice.5301, f32[64]{0:T(128)S(1)} %copy-done.55, f32[2048]{0:T(1024)S(1)} %bitcast.3491, ...), kind=kOutput, calls=%fused_computation.1428 | convolution fusion | flops 2184708096 | bytes 102015488 | tf_op jit(solution)/shard_map/dot_general | solution.py:77
  1838.9 39.9 %reduce-scatter.18.cloned.1.call-done = bf16[4096,512]{1,0:T(8,128)(2,1)} async-done(((bf16[4096,2048]{1,0:T(8,128)(2,1)}), bf16[4096,512]{1,0:T(8,128)(2,1)}) %reduce-scatter.18.cloned.1.call-update) | async-done | bytes 4194320 | tf_op jit(solution)/shard_map/reduce_scatter | solution.py:349
  1885.7 230.7 %reduce-scatter.10.cloned.1.call-done = bf16[2048,2048]{1,0:T(8,128)(2,1)} async-done(((bf16[2048,8192]{1,0:T(8,128)(2,1)}), bf16[2048,2048]{1,0:T(8,128)(2,1)}) %reduce-scatter.10.cloned.1.call-update) | async-done | bytes 8388624 | tf_op jit(solution)/shard_map/reduce_scatter | solution.py:328
  2149.5 15.9 fusion.424
  2165.4 15.9 fusion.419
  2200.4 98.9 %all-reduce.216 = (f32[512]{0:T(512)}, f32[4,1024]{1,0:T(4,128)}, f32[1024]{0:T(1024)}, f32[160,1024]{1,0:T(8,128)}, f32[128,1024]{1,0:T(8,128)}, /*index=5*/f32[1024]{0:T(1024)}, f32[1024]{0:T(1024)}) all-reduce(f32[512]{0:T(512)S(1)} %dynamic-slice_convert_fusion.3, ...), channel_id=1, replica_groups=mesh['replica'=8,'shard'=4] {'replica'}, use_global_device_ids=true, to_apply=%region_227.228 | all-reduce | flops 302592 | bytes 1822720 | tf_op jit(solution)/shard_map/psum | solution.py:357
  2299.3 73.4 %reduce-scatter.20.cloned.1.call-done = f32[512,512]{1,0:T(8,128)} async-done(((f32[4096,512]{1,0:T(8,128)}), f32[512,512]{1,0:T(8,128)}) %reduce-scatter.20.cloned.1.call-update) | async-done | bytes 1048592 | tf_op jit(solution)/shard_map/reduce_scatter | solution.py:355
  2372.8 285.7 %reduce-scatter.12.cloned.1.call-done = f32[256,2048]{1,0:T(8,128)} async-done(((f32[2048,2048]{1,0:T(8,128)}), f32[256,2048]{1,0:T(8,128)}) %reduce-scatter.12.cloned.1.call-update) | async-done | bytes 2097168 | tf_op jit(solution)/shard_map/reduce_scatter | solution.py:354
  (1411 shorter events, 1105.8 us)
Async XLA Ops:
  7.2 275.9 %copy-start.86 = (bf16[512]{0:T(512)(128)(2,1)S(1)}, bf16[512]{0:T(512)(128)(2,1)}, u32[]{:S(2)}) copy-start(bf16[512]{0:T(512)(128)(2,1)} %param.38) | copy-start | bytes 3076
  7.2 378.4 %copy-start.82 = (bf16[1024]{0:T(1024)(128)(2,1)S(1)}, bf16[1024]{0:T(1024)(128)(2,1)}, u32[]{:S(2)}) copy-start(bf16[1024]{0:T(1024)(128)(2,1)} %param.41) | copy-start | bytes 6148
  7.2 386.6 %copy-start.83 = (bf16[1024]{0:T(1024)(128)(2,1)S(1)}, bf16[1024]{0:T(1024)(128)(2,1)}, u32[]{:S(2)}) copy-start(bf16[1024]{0:T(1024)(128)(2,1)} %param.45) | copy-start | bytes 6148
  7.2 392.5 %copy-start.84 = (bf16[1024]{0:T(1024)(128)(2,1)S(1)}, bf16[1024]{0:T(1024)(128)(2,1)}, u32[]{:S(2)}) copy-start(bf16[1024]{0:T(1024)(128)(2,1)} %param.44) | copy-start | bytes 6148
  7.2 397.7 %copy-start.85 = (s32[2,256]{1,0:T(2,128)S(1)}, s32[2,256]{1,0:T(2,128)}, u32[]{:S(2)}) copy-start(s32[2,256]{1,0:T(2,128)} %param.37) | copy-start | bytes 6148
  7.2 399.1 %copy-start.77 = (bf16[4,1024]{1,0:T(4,128)(2,1)S(1)}, bf16[4,1024]{1,0:T(4,128)(2,1)}, u32[]{:S(2)}) copy-start(bf16[4,1024]{1,0:T(4,128)(2,1)} %param.40) | copy-start | bytes 24580
  7.2 404.3 %copy-start.1 = (bf16[2,64,2048]{2,1,0:T(8,128)(2,1)S(1)}, bf16[2,64,2048]{2,1,0:T(8,128)(2,1)}, u32[]{:S(2)}) copy-start(bf16[2,64,2048]{2,1,0:T(8,128)(2,1)} %param.36) | copy-start | bytes 1572868
  7.3 486.3 %all-gather.21.cloned.1.call-start = ((), (), s32[]{:S(2)}) async-start(), calls=%async_computation.9 | async-start | bytes 20971520 | tf_op jit(solution)/shard_map/all_gather | solution.py:314
  8.0 500.9 %all-gather.17.cloned.1.call-start = ((), (), s32[]{:S(2)}) async-start(), calls=%async_computation.7 | async-start | bytes 1638400 | tf_op jit(solution)/shard_map/all_gather | solution.py:310
  8.0 271.0 %collective-permute-start = (bf16[2048,2048]{1,0:T(8,128)(2,1)}, bf16[2048,2048]{1,0:T(8,128)(2,1)}, u32[]{:S(2)}, u32[]{:S(2)}) collective-permute-start(bf16[2048,2048]{1,0:T(8,128)(2,1)} %param.39), channel_id=1, source_target_pairs={{0,1},{1,2},{2,3},{3,0},{4,5},{5,6},{6,7},{7,4},{8,9},{9,10},{10,1... | collective-permute-start | bytes 25165832 | tf_op jit(solution)/shard_map/ppermute | solution.py:19
  8.5 431.4 %collective-permute-start.1 = (bf16[2048,2048]{1,0:T(8,128)(2,1)}, bf16[2048,2048]{1,0:T(8,128)(2,1)}, u32[]{:S(2)}, u32[]{:S(2)}) collective-permute-start(bf16[2048,2048]{1,0:T(8,128)(2,1)} %param.39), channel_id=1, source_target_pairs={{0,3},{1,0},{2,1},{3,2},{4,7},{5,4},{6,5},{7,6},{8,11},{9,8},{10,9... | collective-permute-start | bytes 25165832 | tf_op jit(solution)/shard_map/ppermute | solution.py:22
  279.0 169.1 %collective-permute-start.2 = (bf16[2048,2048]{1,0:T(8,128)(2,1)}, bf16[2048,2048]{1,0:T(8,128)(2,1)}, u32[]{:S(2)}, u32[]{:S(2)}) collective-permute-start(bf16[2048,2048]{1,0:T(8,128)(2,1)} %collective-permute-done), channel_id=1, source_target_pairs={{0,1},{1,2},{2,3},{3,0},{4,5},{5,6},{6,7},{7,4},{8,9},{9,10},{10,1... | collective-permute-start | bytes 25165832 | tf_op jit(solution)/shard_map/ppermute | solution.py:19
  281.6 230.2 %all-gather.19.cloned.1.call-start = ((), (), s32[]{:S(2)}) async-start(), calls=%async_computation.8 | async-start | bytes 1310720 | tf_op jit(solution)/shard_map/all_gather | solution.py:311
  282.3 775.3 %all-gather.23.cloned.1.call-start = ((), (), s32[]{:S(2)}) async-start(), calls=%async_computation.16 | async-start | bytes 1310720 | tf_op jit(solution)/shard_map/all_gather | solution.py:37
  282.5 140.9 %copy-start.50 = (bf16[4,16,16]{2,1,0:T(8,128)(2,1)}, bf16[4,16,16]{2,1,0:T(8,128)(2,1)S(1)}, u32[]{:S(2)}) copy-start(bf16[4,16,16]{2,1,0:T(8,128)(2,1)S(1)} %fusion.626) | copy-start | bytes 6148
  385.6 86.8 %copy-start.39 = (f32[4,1,512]{2,1,0:T(1,128)}, f32[4,1,512]{2,1,0:T(1,128)S(1)}, u32[]{:S(2)}) copy-start(f32[4,1,512]{2,1,0:T(1,128)S(1)} %convert_element_type.375) | copy-start | bytes 24580
  393.8 99.7 %copy-start.64 = (f32[4096]{0:T(1024)}, f32[4096]{0:T(1024)S(1)}, u32[]{:S(2)}) copy-start(f32[4096]{0:T(1024)S(1)} %convert_element_type.292) | copy-start | bytes 49156
  404.9 106.9 %copy-start.62 = (f32[4096]{0:T(1024)}, f32[4096]{0:T(1024)S(1)}, u32[]{:S(2)}) copy-start(f32[4096]{0:T(1024)S(1)} %convert_element_type.305) | copy-start | bytes 49156
  411.8 44.6 %copy-start.56 = (f32[64]{0:T(128)}, f32[64]{0:T(128)S(1)}, u32[]{:S(2)}) copy-start(f32[64]{0:T(128)S(1)} %add_rsqrt_fusion.1) | copy-start | bytes 772
  411.8 60.7 %copy-start.54 = (f32[64]{0:T(128)}, f32[64]{0:T(128)S(1)}, u32[]{:S(2)}) copy-start(f32[64]{0:T(128)S(1)} %add_rsqrt_fusion) | copy-start | bytes 772
  412.5 81.1 %copy-start.87 = (f32[64]{0:T(128)}, f32[64]{0:T(128)S(1)}, u32[]{:S(2)}) copy-start(f32[64]{0:T(128)S(1)} %get-tuple-element.3214) | copy-start | bytes 772
  412.5 81.1 %copy-start.89 = (f32[64]{0:T(128)}, f32[64]{0:T(128)S(1)}, u32[]{:S(2)}) copy-start(f32[64]{0:T(128)S(1)} %get-tuple-element.3217) | copy-start | bytes 772
  412.5 81.1 %copy-start.91 = (f32[64]{0:T(128)}, f32[64]{0:T(128)S(1)}, u32[]{:S(2)}) copy-start(f32[64]{0:T(128)S(1)} %get-tuple-element.3218) | copy-start | bytes 772
  431.7 61.9 %copy-start.69 = (f32[1,4096]{1,0:T(1,128)}, f32[1,4096]{1,0:T(1,128)S(1)}, u32[]{:S(2)}) copy-start(f32[1,4096]{1,0:T(1,128)S(1)} %get-tuple-element.3206) | copy-start | bytes 49156
  431.7 61.9 %copy-start.71 = (f32[1,4096]{1,0:T(1,128)}, f32[1,4096]{1,0:T(1,128)S(1)}, u32[]{:S(2)}) copy-start(f32[1,4096]{1,0:T(1,128)S(1)} %get-tuple-element.3207) | copy-start | bytes 49156
  431.7 61.9 %copy-start.73 = (f32[1,4096]{1,0:T(1,128)}, f32[1,4096]{1,0:T(1,128)S(1)}, u32[]{:S(2)}) copy-start(f32[1,4096]{1,0:T(1,128)S(1)} %get-tuple-element.3208) | copy-start | bytes 49156
  431.7 61.9 %copy-start.75 = (f32[1,4096]{1,0:T(1,128)}, f32[1,4096]{1,0:T(1,128)S(1)}, u32[]{:S(2)}) copy-start(f32[1,4096]{1,0:T(1,128)S(1)} %get-tuple-element.3209) | copy-start | bytes 49156
  470.2 21.0 collective-permute-start.3
  487.3 5.1 collective-permute-start.4
  675.7 384.8 %all-gather.25.cloned.1.call-start = ((), (), s32[]{:S(2)}) async-start(), calls=%async_computation.17 | async-start | bytes 1310720 | tf_op jit(solution)/shard_map/all_gather | solution.py:37
  942.2 95.5 %copy-start.5 = (f32[4096,16]{0,1:T(8,128)}, f32[4096,16]{0,1:T(8,128)S(1)}, u32[]{:S(2)}) copy-start(f32[4096,16]{0,1:T(8,128)S(1)} %get-tuple-element.1341) | copy-start | bytes 786436
  942.9 74.7 %copy-start.7 = (f32[4096,16]{0,1:T(8,128)S(1)}, f32[4096,16]{0,1:T(8,128)}, u32[]{:S(2)}) copy-start(f32[4096,16]{0,1:T(8,128)} %copy-done.6) | copy-start | bytes 786436
  1034.4 365.9 %all-gather.27.cloned.1.call-start = ((), (), s32[]{:S(2)}) async-start(), calls=%async_computation.18 | async-start | bytes 1310720 | tf_op jit(solution)/shard_map/all_gather | solution.py:37
  1054.2 349.1 %all-gather.29.cloned.1.call-start = ((), (), s32[]{:S(2)}) async-start(), calls=%async_computation.19 | async-start | bytes 1310720 | tf_op jit(solution)/shard_map/all_gather | solution.py:37
  1057.6 821.2 %reduce-scatter.18.cloned.1.call-start = ((), (), s32[]{:S(2)}) async-start(), calls=%async_computation.14 | async-start | bytes 20971520 | tf_op jit(solution)/shard_map/reduce_scatter | solution.py:349
  1521.9 191.8 %copy-start.14 = (bf16[64,4096]{1,0:T(8,128)(2,1)S(1)}, bf16[64,4096]{1,0:T(8,128)(2,1)}, u32[]{:S(2)}) copy-start(bf16[64,4096]{1,0:T(8,128)(2,1)} %copy-done.13) | copy-start | bytes 1572868
  1521.9 191.9 %copy-start.53 = (f32[4096]{0:T(1024)S(1)}, f32[4096]{0:T(1024)}, u32[]{:S(2)}) copy-start(f32[4096]{0:T(1024)} %convert_element_type.309) | copy-start | bytes 49156
  1752.5 363.9 %reduce-scatter.10.cloned.1.call-start = ((), (), s32[]{:S(2)}) async-start(), calls=%async_computation.10 | async-start | bytes 41943040 | tf_op jit(solution)/shard_map/reduce_scatter | solution.py:328
  1760.1 6.8 collective-permute-start.6
  1765.3 30.4 %copy-start.28 = (bf16[61,4096]{1,0:T(8,128)(2,1)}, bf16[61,4096]{1,0:T(8,128)(2,1)S(1)}, u32[]{:S(2)}) copy-start(bf16[61,4096]{1,0:T(8,128)(2,1)S(1)} %slice.5301) | copy-start | bytes 1499140
  1765.5 30.2 %copy-start.26 = (bf16[61,4096]{1,0:T(8,128)(2,1)}, bf16[61,4096]{1,0:T(8,128)(2,1)S(1)}, u32[]{:S(2)}) copy-start(bf16[61,4096]{1,0:T(8,128)(2,1)S(1)} %slice.5298) | copy-start | bytes 1499140
  1765.5 3.8 collective-permute-start.5
  1769.3 26.4 copy-start.24
  1829.8 363.3 %reduce-scatter.22.cloned.1.call-start = ((), (), s32[]{:S(2)}) async-start(), calls=%async_computation.20 | async-start | bytes 1310720
  1833.5 360.6 %reduce-scatter.16.cloned.1.call-start = ((), (), s32[]{:S(2)}) async-start(), calls=%async_computation.13 | async-start | bytes 1310720 | tf_op jit(solution)/shard_map/reduce_scatter | solution.py:340
  1836.1 364.3 %reduce-scatter.14.cloned.1.call-start = ((), (), s32[]{:S(2)}) async-start(), calls=%async_computation.12 | async-start | bytes 1638400 | tf_op jit(solution)/shard_map/reduce_scatter | solution.py:337
  1838.8 533.9 %reduce-scatter.20.cloned.1.call-start = ((), (), s32[]{:S(2)}) async-start(), calls=%async_computation.15 | async-start | bytes 9437184 | tf_op jit(solution)/shard_map/reduce_scatter | solution.py:355
  1885.4 773.1 %reduce-scatter.12.cloned.1.call-start = ((), (), s32[]{:S(2)}) async-start(), calls=%async_computation.11 | async-start | bytes 18874368 | tf_op jit(solution)/shard_map/reduce_scatter | solution.py:354
  (78 other events, 419.6 us)
Sparse Core Ops, SparseCore 0:
  9.6 198.6 all-gather.20
  281.7 23.4 all-gather.16
  306.8 19.5 all-gather.18
  675.8 17.6 all-gather.22
  1034.5 17.5 all-gather.24
  1054.3 16.7 all-gather.26
  1072.7 16.7 all-gather.28
  1752.7 126.0 reduce-scatter.17
  1881.5 234.7 reduce-scatter.9
  2118.9 24.8 reduce-scatter.21
  2146.4 24.8 reduce-scatter.15
  2173.8 26.5 reduce-scatter.13
  2204.6 168.1 reduce-scatter.19
  2377.4 281.0 reduce-scatter.11
